TPU v7x, 512 devices: a whole 4x4x16 slice. The times are simulated.
512 devices in a mesh: seq: 64 (over y, z), mp: 8 (over x, core).
Axes of the slice: x: 4, y: 4, z: 16, core: 2. Of those that a mesh axis runs over, the one named last changes fastest.
Arguments:
- byte_states: bfloat16 [16384, 1024], P('seq'), may hold values from -6 to 6
- outer_gain: float32 [1024], replicated, may hold values from 0.1 to 1.9
- mamba_input: bfloat16 [1024, 1024], P(None, 'mp'), may hold values from -0.1875 to 0.1875
- mamba_step: bfloat16 [1024, 1024], P(None, 'mp'), may hold values from -0.1875 to 0.1875
- decay_rate: float32 [1024], P('mp'), as said below
- mixer_weight: bfloat16 [1024, 1024], P('mp'), may hold values from -0.1875 to 0.1875
- boundaries: int32 [64, 128], P('seq'), may hold values from 0 to 256, as said below
- span_counts: int32 [64], replicated, may hold values from 1 to 128, as said below
- up_weight: bfloat16 [1024, 4096], P('seq', 'mp'), may hold values from -0.1875 to 0.1875
- up_bias: float32 [4096], P('mp'), may hold values from -5 to 5
- inner_gain: float32 [4096], replicated, as said below
- query_weight: bfloat16 [4096, 4096], P('seq', 'mp'), as said below
- key_weight: bfloat16 [4096, 1024], P('seq', 'mp'), as said below
- value_weight: bfloat16 [4096, 1024], P('seq', 'mp'), may hold values from -0.09375 to 0.09375
- return_weight: bfloat16 [4096, 1024], P('mp'), may hold values from -0.09375 to 0.09375
Outputs:
- joined: bfloat16 [16384, 1024], P('seq', 'mp')
Inputs may be any that keep to these rules, and one draw needn't show every extreme that they name: `boundaries`: row s lists the spans of shard s: its first span_counts[s] entries rise strictly from 0 and are byte positions within the shard; each span runs to the next entry, the last to the shard's end; the other entries equal 256. `span_counts`: the counts sum to 4096; some shard has exactly 128 spans. `decay_rate`: Positive. `inner_gain`: Positive. `query_weight`: Finite. `key_weight`: Finite.
All inputs are finite; a program needn't handle non-finite values.
Results may differ from a plain program's by a relative error of at most 0.01.
Values may be sent and summed in bfloat16 or wider, within the bound.
A program may use at most 64 MiB of HBM per device.

v0:
```python
import math
import jax
import jax.numpy as jnp
from jax import lax
from jax.sharding import PartitionSpec as P

HEADS = 32
KV_HEADS = 8
HEAD = 128
eps = 1e-05
masked = -1e30
far_index = 1073741824


def prefix(value, axis, join, neutral):
    count, mine = (lax.axis_size(axis), lax.axis_index(axis))
    pieces = jax.tree.map(lambda part: lax.all_gather(part, axis), value)
    so_far = jax.tree.map(
        lambda part, zero: jnp.full_like(part, 0) + jnp.asarray(zero, part.dtype), value, neutral
    )

    def lap(position, so_far):
        longer = join(so_far, jax.tree.map(lambda part: part[position], pieces))
        return jax.tree.map(lambda new, old: jnp.where(position < mine, new, old), longer, so_far)

    return lax.fori_loop(0, count - 1, lap, so_far)


def rms_scale(values, gain):
    values = values.astype(jnp.float32)
    return values * lax.rsqrt(jnp.mean(values * values, axis=-1, keepdims=True) + eps) * gain


def combine_pairs(earlier, later):
    return (earlier[0] * later[0], later[0] * earlier[1] + later[1])


def pick_table(table, wanted, seq_ids):
    return jnp.sum(jnp.where(seq_ids[None, :] == wanted[:, None], table[None, :], 0), axis=1)


def block_size(piece_rows, shard_rows):
    limit = max(1, 1024 // shard_rows)
    pieces = max(1, piece_rows // shard_rows)
    best_size = 1
    for candidate in range(1, limit + 1):
        if pieces % candidate == 0:
            best_size = candidate
    return min(piece_rows, best_size * shard_rows)


def on_device(
    byte_states,
    outer_gain,
    mamba_input,
    mamba_step,
    decay_rate,
    mixer_weight,
    boundaries,
    span_counts,
    up_weight,
    up_bias,
    inner_gain,
    query_weight,
    key_weight,
    value_weight,
    return_weight,
):
    shards = lax.axis_size("seq")
    own_shard = lax.axis_index("seq")
    own_lane = lax.axis_index("mp")
    rows_here = byte_states.shape[0]
    capacity = boundaries.shape[1]
    column_count = mamba_input.shape[1]
    kv_local = key_weight.shape[1] // HEAD
    group_size = HEADS // KV_HEADS
    offsets = jnp.cumsum(span_counts) - span_counts
    seq_ids = jnp.arange(shards, dtype=jnp.int32)
    own_offset = jnp.sum(jnp.where(seq_ids == own_shard, offsets, 0))
    own_count = jnp.sum(jnp.where(seq_ids == own_shard, span_counts, 0))
    normed = rms_scale(byte_states, outer_gain).astype(jnp.bfloat16)
    inputs = jnp.dot(normed, mamba_input, preferred_element_type=jnp.float32)
    step_sizes = jax.nn.softplus(jnp.dot(normed, mamba_step, preferred_element_type=jnp.float32))
    rate_steps = step_sizes * decay_rate
    decays = jnp.exp(-rate_steps)
    drives = jnp.sqrt(-jnp.expm1(-2.0 * rate_steps)) * inputs
    through, local_states = lax.associative_scan(combine_pairs, (decays, drives), axis=0)
    starting = (jnp.ones((column_count,), jnp.float32), jnp.zeros((column_count,), jnp.float32))
    arriving = prefix((through[-1], local_states[-1]), "seq", combine_pairs, starting)
    states = (local_states + through * arriving[1][None, :]).astype(jnp.bfloat16)
    partial_value = jnp.dot(states, mixer_weight, preferred_element_type=jnp.float32)
    mixed_sum = lax.psum(partial_value, "mp")
    encoded = (byte_states.astype(jnp.float32) + mixed_sum).astype(jnp.bfloat16)
    skip_part = lax.dynamic_slice_in_dim(encoded, own_lane * column_count, column_count, 1)
    own_marks = boundaries[0]
    pooled = encoded[jnp.minimum(own_marks, rows_here - 1)]
    local_slot = jnp.arange(capacity, dtype=jnp.int32)
    query_index = jnp.where(local_slot < own_count, own_offset + local_slot, -1)
    columns = pooled
    widened_sum = jnp.dot(
        columns,
        lax.all_gather(up_weight, "seq", axis=0, tiled=True),
        preferred_element_type=jnp.float32,
    )
    widened_share = (widened_sum + up_bias[None, :]).astype(jnp.bfloat16)
    widened = lax.all_gather(widened_share, "mp", axis=1, tiled=True)
    inner_normed = rms_scale(widened, inner_gain).astype(jnp.bfloat16)
    columns = inner_normed
    query_part = jnp.dot(
        columns,
        lax.all_gather(query_weight, "seq", axis=0, tiled=True),
        preferred_element_type=jnp.float32,
    )
    key_part = jnp.dot(
        columns,
        lax.all_gather(key_weight, "seq", axis=0, tiled=True),
        preferred_element_type=jnp.float32,
    )
    value_part = jnp.dot(
        columns,
        lax.all_gather(value_weight, "seq", axis=0, tiled=True),
        preferred_element_type=jnp.float32,
    )
    queries = query_part.astype(jnp.bfloat16)
    key_rows = key_part.astype(jnp.bfloat16)
    value_rows = value_part.astype(jnp.bfloat16)
    query_count = queries.shape[0]
    grouped = (
        queries.reshape(query_count, kv_local, group_size, HEAD)
        .transpose(1, 0, 2, 3)
        .reshape(kv_local, query_count * group_size, HEAD)
    )
    row_index = jnp.repeat(query_index, group_size)
    shard_rows = key_rows.shape[0]
    score_scale = 1.0 / math.sqrt(HEAD)

    def key_index(whole_index):
        holder = whole_index // shard_rows
        within = whole_index % shard_rows
        holder_offset = pick_table(offsets, holder, seq_ids)
        holder_count = pick_table(span_counts, holder, seq_ids)
        return jnp.where(within < holder_count, holder_offset + within, far_index)

    def attend_block(running, key_block, value_block, index_block):
        row_peak, denominator, weighted = running
        scores = (
            jnp.einsum("hqd,khd->hqk", grouped, key_block, preferred_element_type=jnp.float32)
            * score_scale
        )
        scores = jnp.where(index_block[None, None, :] <= row_index[None, :, None], scores, masked)
        new_peak = jnp.maximum(row_peak, jnp.max(scores, axis=2))
        shrink = jnp.exp(row_peak - new_peak)
        lifted = jnp.exp(scores - new_peak[:, :, None])
        denominator = denominator * shrink + jnp.sum(lifted, axis=2)
        weighted = weighted * shrink[:, :, None] + jnp.einsum(
            "hqk,khd->hqd",
            lifted.astype(jnp.bfloat16),
            value_block,
            preferred_element_type=jnp.float32,
        )
        return (new_peak, denominator, weighted)

    query_total = query_count * group_size
    initial = (
        jnp.full((kv_local, query_total), masked, jnp.float32),
        jnp.zeros((kv_local, query_total), jnp.float32),
        jnp.zeros((kv_local, query_total, HEAD), jnp.float32),
    )
    key_piece = lax.all_gather(key_rows, "seq", axis=0, tiled=True)
    value_piece = lax.all_gather(value_rows, "seq", axis=0, tiled=True)
    piece_rows = key_piece.shape[0]
    block_rows = block_size(piece_rows, shard_rows)
    turn_count = piece_rows // block_rows
    key_blocks = key_piece.reshape(turn_count, block_rows, kv_local, HEAD)
    value_blocks = value_piece.reshape(turn_count, block_rows, kv_local, HEAD)

    def one_turn(turn_index, inner_running):
        whole_index = turn_index * block_rows + jnp.arange(block_rows, dtype=jnp.int32)
        return attend_block(
            inner_running, key_blocks[turn_index], value_blocks[turn_index], key_index(whole_index)
        )

    row_peak, denominator, weighted = lax.fori_loop(0, turn_count, one_turn, initial)
    attended = (weighted / denominator[:, :, None]).astype(jnp.bfloat16)
    attended = (
        attended.reshape(kv_local, query_count, group_size, HEAD)
        .transpose(1, 0, 2, 3)
        .reshape(query_count, kv_local * group_size * HEAD)
    )
    projected = jnp.dot(attended, return_weight, preferred_element_type=jnp.float32)
    returned = lax.psum_scatter(
        projected.astype(jnp.bfloat16), "mp", scatter_dimension=1, tiled=True
    )
    positions = jnp.arange(rows_here, dtype=jnp.int32)
    live_slots = jnp.arange(capacity, dtype=jnp.int32) < own_count
    passed = jnp.sum(
        ((own_marks[None, :] <= positions[:, None]) & live_slots[None, :]).astype(jnp.int32), axis=1
    )
    return (skip_part.astype(jnp.float32) + returned[passed - 1].astype(jnp.float32)).astype(
        jnp.bfloat16
    )


def solution(mesh):
    in_specs = (
        P("seq", None),
        P(),
        P(None, "mp"),
        P(None, "mp"),
        P("mp"),
        P("mp", None),
        P("seq", None),
        P(),
        P("seq", "mp"),
        P("mp"),
        P(),
        P("seq", "mp"),
        P("seq", "mp"),
        P("seq", "mp"),
        P("mp", None),
    )
    out_specs = P("seq", "mp")
    return jax.shard_map(
        on_device, mesh=mesh, in_specs=in_specs, out_specs=out_specs, check_vma=False
    )
```

profile of v0, /device:TPU:8, one launch (start us, length us, event | category | flops | bytes accessed | tf_op | source)
XLA Modules:
  0.0 1139.2 jit_solution(18261109659851616036)
XLA Ops:
  7.4 1.3 fusion.32
  8.8 1.5 negate_exponential_fusion
  12.6 79.6 %all-gather.1 = f32[64,1,128]{2,1,0:T(1,128)S(1)} all-gather(f32[1,1,128]{2,1,0:T(1,128)S(1)} %add_bitcast_fusion), channel_id=1, replica_groups=mesh['seq'=64,'mp'=8] {'seq'}, dimensions={0}, use_global_device_ids=true | all-gather | bytes 33280 | tf_op jit(solution)/shard_map/all_gather | solution.py:17
  92.3 73.3 %all-gather = f32[64,1,128]{2,1,0:T(1,128)S(1)} all-gather(f32[1,1,128]{2,1,0:T(1,128)S(1)} %add_bitcast_fusion.1), channel_id=1, replica_groups=mesh['seq'=64,'mp'=8] {'seq'}, dimensions={0}, use_global_device_ids=true | all-gather | bytes 33280 | tf_op jit(solution)/shard_map/all_gather | solution.py:17
  165.6 2.6 while.34
  168.2 1.3 fusion.43
  170.2 73.0 %all-reduce.34.cloned.1.call-done = f32[256,1024]{1,0:T(8,128)} async-done(((f32[256,1024]{1,0:T(8,128)}), f32[256,1024]{1,0:T(8,128)}) %all-reduce.34.cloned.1.call-update) | async-done | bytes 1048592 | tf_op jit(solution)/shard_map/psum | solution.py:92
  243.2 1.4 fusion.35
  244.6 0.9 gather_fusion
  245.5 61.3 %all-gather.10.cloned.1.call-done = bf16[1024,512]{1,0:T(8,128)(2,1)} async-done(((bf16[16,512]{1,0:T(8,128)(2,1)}), bf16[1024,512]{1,0:T(8,128)(2,1)}) %all-gather.10.cloned.1.call-update) | async-done | bytes 1048592 | tf_op jit(solution)/shard_map/all_gather | solution.py:102
  306.7 2.2 fusion.31
  310.9 26.2 %all-gather.12.cloned.1.call-done = bf16[128,4096]{1,0:T(8,128)(2,1)} async-done(((bf16[128,512]{1,0:T(8,128)(2,1)}), bf16[128,4096]{1,0:T(8,128)(2,1)}) %all-gather.12.cloned.1.call-update) | async-done | bytes 1048592 | tf_op jit(solution)/shard_map/all_gather | solution.py:106
  337.1 1.6 fusion.28
  338.8 140.2 %all-gather.20.cloned.1.call-done = bf16[4096,128]{1,0:T(8,128)(2,1)} async-done(((bf16[64,128]{1,0:T(8,128)(2,1)}), bf16[4096,128]{1,0:T(8,128)(2,1)}) %all-gather.20.cloned.1.call-update) | async-done | bytes 1048592 | tf_op jit(solution)/shard_map/all_gather | solution.py:121
  478.9 2.7 convolution_convert_fusion.2
  481.7 136.0 %all-gather.14.cloned.1.call-done = bf16[4096,128]{1,0:T(8,128)(2,1)} async-done(((bf16[64,128]{1,0:T(8,128)(2,1)}), bf16[4096,128]{1,0:T(8,128)(2,1)}) %all-gather.14.cloned.1.call-update) | async-done | bytes 1048592 | tf_op jit(solution)/shard_map/all_gather | solution.py:116
  617.7 2.3 convolution_convert_fusion.3
  620.5 1.3 fusion.50
  622.5 1.9 add_select_fusion.3
  625.1 137.2 %all-gather.18.cloned.1.call-done = bf16[4096,512]{1,0:T(8,128)(2,1)} async-done(((bf16[64,512]{1,0:T(8,128)(2,1)}), bf16[4096,512]{1,0:T(8,128)(2,1)}) %all-gather.18.cloned.1.call-update) | async-done | bytes 4194320 | tf_op jit(solution)/shard_map/all_gather | solution.py:111
  762.2 3.0 convolution_convert_fusion.1
  765.3 135.9 %all-gather.22.cloned.1.call-done = bf16[8192,128]{1,0:T(8,128)(2,1)} async-done(((bf16[128,128]{1,0:T(8,128)(2,1)}), bf16[8192,128]{1,0:T(8,128)(2,1)}) %all-gather.22.cloned.1.call-update) | async-done | bytes 2097168 | tf_op jit(solution)/shard_map/all_gather | solution.py:170
  901.2 140.0 %all-gather.16.cloned.1.call-done = bf16[8192,128]{1,0:T(8,128)(2,1)} async-done(((bf16[128,128]{1,0:T(8,128)(2,1)}), bf16[8192,128]{1,0:T(8,128)(2,1)}) %all-gather.16.cloned.1.call-update) | async-done | bytes 2097168 | tf_op jit(solution)/shard_map/all_gather | solution.py:169
  1041.2 50.0 %while.35 = (s32[]{:T(128)}, f32[1,512]{1,0:T(1,128)S(1)}, f32[1,512]{1,0:T(1,128)S(1)}, f32[1,512,128]{2,1,0:T(8,128)S(1)}, s32[64]{0:T(128)S(1)}, /*index=5*/s...) while((s32[]{:T(128)}, f32[1,512]{1,0:T(1,128)S(1)}, ...), condition=%wide.region_13.14_spmd.clone, body=%wide.region_8.13_spmd.clone.sunk | while | flops 273186304 | bytes 7548097 | solution.py:183
  1041.2 0.8 fusion.77
  1042.9 2.0 fusion.78
  1046.0 1.5 fusion.82
  1047.5 0.8 fusion.77
  1049.2 2.0 fusion.78
  1052.2 1.5 fusion.82
  1053.7 0.8 fusion.77
  1055.4 2.0 fusion.78
  1058.5 1.5 fusion.82
  1061.7 2.0 fusion.78
  1064.7 1.5 fusion.82
  1067.9 2.0 fusion.78
  1071.0 1.5 fusion.82
  1074.1 2.0 fusion.78
  1077.2 1.5 fusion.82
  1080.4 2.0 fusion.78
  1083.5 1.5 fusion.82
  1086.6 2.0 fusion.78
  1089.7 1.5 fusion.82
  1091.8 0.8 copy.28
  1092.7 35.8 %reduce-scatter.4.cloned.1.call-done = bf16[128,128]{1,0:T(8,128)(2,1)} async-done(((bf16[1024,128]{1,0:T(8,128)(2,1)}), bf16[128,128]{1,0:T(8,128)(2,1)}) %reduce-scatter.4.cloned.1.call-update) | async-done | bytes 32784
  1128.5 0.9 copy.29
  1129.4 0.9 gather_fusion.1
  1130.3 1.5 add_convert_fusion
  (335 shorter events, 27.5 us)
Async XLA Ops:
  7.4 1084.1 %copy-start = (bf16[512,1024]{1,0:T(8,128)(2,1)S(1)}, bf16[512,1024]{1,0:T(8,128)(2,1)}, u32[]{:S(2)}) copy-start(bf16[512,1024]{1,0:T(8,128)(2,1)} %param.33) | copy-start | bytes 3145732
  7.4 3.0 copy-start.2
  7.4 3.0 copy-start.12
  7.4 3.0 copy-start.10
  7.4 235.8 %all-reduce.34.cloned.1.call-start = ((), (), s32[]{:S(2)}) async-start(), calls=%async_computation.1 | async-start | bytes 2097152 | tf_op jit(solution)/shard_map/psum | solution.py:92
  11.7 156.5 %copy-start.4 = (bf16[128,1024]{1,0:T(8,128)(2,1)S(1)}, bf16[128,1024]{1,0:T(8,128)(2,1)}, u32[]{:S(2)}) copy-start(bf16[128,1024]{1,0:T(8,128)(2,1)} %param.24) | copy-start | bytes 786436
  12.5 157.6 %copy-start.9 = (s32[1,128]{1,0:T(1,128)S(1)}, s32[1,128]{1,0:T(1,128)}, u32[]{:S(2)}) copy-start(s32[1,128]{1,0:T(1,128)} %param.25) | copy-start | bytes 1540
  169.5 137.2 %all-gather.10.cloned.1.call-start = ((), (), s32[]{:S(2)}) async-start(), calls=%async_computation.2 | async-start | bytes 1064960 | tf_op jit(solution)/shard_map/all_gather | solution.py:102
  170.1 167.0 %all-gather.12.cloned.1.call-start = ((), (), s32[]{:S(2)}) async-start(), calls=%async_computation.3 | async-start | bytes 1179648 | tf_op jit(solution)/shard_map/all_gather | solution.py:106
  170.2 136.5 %copy-start.8 = (f32[512]{0:T(512)S(1)}, f32[512]{0:T(512)}, u32[]{:S(2)}) copy-start(f32[512]{0:T(512)} %param.28) | copy-start | bytes 6148
  244.6 94.2 %copy-start.1 = (bf16[256,1024]{1,0:T(8,128)(2,1)}, bf16[256,1024]{1,0:T(8,128)(2,1)S(1)}, u32[]{:S(2)}) copy-start(bf16[256,1024]{1,0:T(8,128)(2,1)S(1)} %fusion.35) | copy-start | bytes 1572868
  244.6 234.3 %copy-start.11 = (f32[4096]{0:T(1024)S(1)}, f32[4096]{0:T(1024)}, u32[]{:S(2)}) copy-start(f32[4096]{0:T(1024)} %param.29) | copy-start | bytes 49156
  309.0 170.0 %all-gather.20.cloned.1.call-start = ((), (), s32[]{:S(2)}) async-start(), calls=%async_computation.7 | async-start | bytes 1064960 | tf_op jit(solution)/shard_map/all_gather | solution.py:121
  309.7 308.0 %all-gather.14.cloned.1.call-start = ((), (), s32[]{:S(2)}) async-start(), calls=%async_computation.4 | async-start | bytes 1064960 | tf_op jit(solution)/shard_map/all_gather | solution.py:116
  310.3 452.0 %all-gather.18.cloned.1.call-start = ((), (), s32[]{:S(2)}) async-start(), calls=%async_computation.6 | async-start | bytes 4259840 | tf_op jit(solution)/shard_map/all_gather | solution.py:111
  310.9 590.4 %all-gather.22.cloned.1.call-start = ((), (), s32[]{:S(2)}) async-start(), calls=%async_computation.8 | async-start | bytes 2129920 | tf_op jit(solution)/shard_map/all_gather | solution.py:170
  337.1 280.6 %copy-start.3 = (bf16[128,4096]{1,0:T(8,128)(2,1)S(1)}, bf16[128,4096]{1,0:T(8,128)(2,1)}, u32[]{:S(2)}) copy-start(bf16[128,4096]{1,0:T(8,128)(2,1)} %all-gather.12.cloned.1.call-done) | copy-start | bytes 3145732
  338.8 281.4 %copy-start.5 = (s32[64]{0:T(128)S(1)}, s32[64]{0:T(128)}, u32[]{:S(2)}) copy-start(s32[64]{0:T(128)} %param.26) | copy-start | bytes 772
  481.6 559.6 %all-gather.16.cloned.1.call-start = ((), (), s32[]{:S(2)}) async-start(), calls=%async_computation.5 | async-start | bytes 2129920 | tf_op jit(solution)/shard_map/all_gather | solution.py:169
  620.1 508.4 %reduce-scatter.4.cloned.1.call-start = ((), (), s32[]{:S(2)}) async-start(), calls=%async_computation.9 | async-start | bytes 294912
  1045.6 1.9 copy-start.6
  1051.8 1.9 copy-start.6
  1058.1 1.9 copy-start.6
  1064.3 1.9 copy-start.6
  1070.6 1.9 copy-start.6
  1076.8 1.9 copy-start.6
  1083.1 1.9 copy-start.6
  1089.3 1.9 copy-start.6
  1091.2 1.4 copy-start.7
Sparse Core Ops, SparseCore 0:
  169.7 73.5 all-reduce.33
  309.1 27.9 all-gather.11
  340.1 138.8 all-gather.19
  481.7 135.9 all-gather.13
  620.5 141.6 all-gather.17
  765.0 136.1 all-gather.21
  904.2 137.0 all-gather.15
  1092.8 35.7 reduce-scatter.3
Sparse Core Ops, SparseCore 1:
  173.0 133.7 all-gather.9
where the time goes:
time: 1140 us
  waiting for transfers between devices  888 us (78%)
  blocking collectives  153 us (13%)
  matrix products  41.2 us (4%)
  other arithmetic  27.3 us (2%)
  between operations  15.9 us (1%)
  local copies, waits for them, and re-layouts  11.6 us (1%)
    all_gather x2, blocking collectives, prefix(): pieces = jax.tree.map(lambda part: lax.all_gather(part, axis), value)  153 us
    all_gather x1, waiting for transfers between devices, on_device(): lax.all_gather(value_weight, 'seq', axis=0, tiled=True)  140 us
    all_gather x1, waiting for transfers between devices, on_device(): key_piece = lax.all_gather(key_rows, 'seq', axis=0, tiled=True)  140 us
    all_gather x1, waiting for transfers between devices, on_device(): lax.all_gather(query_weight, 'seq', axis=0, tiled=True)  137 us
    all_gather x1, waiting for transfers between devices, on_device(): lax.all_gather(key_weight, 'seq', axis=0, tiled=True)  136 us
    all_gather x1, waiting for transfers between devices, on_device(): value_piece = lax.all_gather(value_rows, 'seq', axis=0, tiled=True)  136 us
    psum x1, waiting for transfers between devices, on_device(): mixed_sum = lax.psum(partial_value, 'mp')  73 us
    all_gather x1, waiting for transfers between devices, on_device(): lax.all_gather(up_weight, 'seq', axis=0, tiled=True)  61.3 us
  transfers between devices with their start and end apart: 9, of which 9 were waited for; matrix products, arithmetic and copies ran while one was open for 1% of the time, Pallas kernels for 0%

commit v1 on v0

--- a/solution.py
+++ b/solution.py
@@ -113,7 +113,9 @@
     )
     key_part = jnp.dot(
         columns,
-        lax.all_gather(key_weight, "seq", axis=0, tiled=True),
+        jnp.concatenate(
+            lax.all_to_all(jnp.stack([key_weight] * lax.axis_size("seq")), "seq", 0, 0), axis=0
+        ),
         preferred_element_type=jnp.float32,
     )
     value_part = jnp.dot(

time: 1140 us -> 1000 us (0.88)
  waiting for transfers between devices: 888 us -> 737 us
  starting transfers between devices: 0.36 us -> 11.8 us
    all_gather x1 -> x0, waiting for transfers between devices: 136 us -> none  [on_device(): lax.all_gather(key_weight, 'seq', axis=0, tiled=True)]
    all_gather x1, waiting for transfers between devices: 26.2 us -> 13.9 us  [on_device(): widened = lax.all_gather(widened_share, 'mp', axis=1, tiled=True)]
    all_to_all x0 -> x1, starting transfers between devices: none -> 11.5 us  [on_device(): lax.all_to_all(jnp.stack([key_weight] * lax.axis_size('seq')), 'seq', 0, 0)]
    unnamed x10 -> x9, waiting for transfers between devices: 38.2 us -> 37.6 us
  transfers between devices with their start and end apart: 9 -> 9, of which waited for: 9 -> 8; matrix products, arithmetic and copies ran while one was open for 1% -> 2% of each run, Pallas kernels for 0% -> 0%
where the time goes in v1:
time: 1000 us
  waiting for transfers between devices  737 us (74%)
  blocking collectives  153 us (15%)
  matrix products  40 us (4%)
  other arithmetic  27.3 us (3%)
  between operations  15.9 us (2%)
  local copies, waits for them, and re-layouts  12.9 us (1%)
  starting transfers between devices  11.8 us (1%)
    all_gather x2, blocking collectives, prefix(): pieces = jax.tree.map(lambda part: lax.all_gather(part, axis), value)  153 us
    all_gather x1, waiting for transfers between devices, on_device(): lax.all_gather(value_weight, 'seq', axis=0, tiled=True)  140 us
    all_gather x1, waiting for transfers between devices, on_device(): key_piece = lax.all_gather(key_rows, 'seq', axis=0, tiled=True)  140 us
    all_gather x1, waiting for transfers between devices, on_device(): value_piece = lax.all_gather(value_rows, 'seq', axis=0, tiled=True)  136 us
    all_gather x1, waiting for transfers between devices, on_device(): lax.all_gather(query_weight, 'seq', axis=0, tiled=True)  136 us
    psum x1, waiting for transfers between devices, on_device(): mixed_sum = lax.psum(partial_value, 'mp')  73 us
    all_gather x1, waiting for transfers between devices, on_device(): lax.all_gather(up_weight, 'seq', axis=0, tiled=True)  61.3 us
    unnamed x9, waiting for transfers between devices  37.6 us
  transfers between devices with their start and end apart: 9, of which 8 were waited for; matrix products, arithmetic and copies ran while one was open for 2% of the time, Pallas kernels for 0%

profile of v1, /device:TPU:8, one launch (start us, length us, event | category | flops | bytes accessed | tf_op | source)
XLA Modules:
  0.0 1000.2 jit_solution(7926342078974162280)
XLA Ops:
  7.4 1.3 fusion.32
  8.8 1.5 negate_exponential_fusion
  12.6 79.6 %all-gather.1 = f32[64,1,128]{2,1,0:T(1,128)S(1)} all-gather(f32[1,1,128]{2,1,0:T(1,128)S(1)} %add_bitcast_fusion), channel_id=1, replica_groups=mesh['seq'=64,'mp'=8] {'seq'}, dimensions={0}, use_global_device_ids=true | all-gather | bytes 33280 | tf_op jit(solution)/shard_map/all_gather | solution.py:17
  92.3 73.3 %all-gather = f32[64,1,128]{2,1,0:T(1,128)S(1)} all-gather(f32[1,1,128]{2,1,0:T(1,128)S(1)} %add_bitcast_fusion.1), channel_id=1, replica_groups=mesh['seq'=64,'mp'=8] {'seq'}, dimensions={0}, use_global_device_ids=true | all-gather | bytes 33280 | tf_op jit(solution)/shard_map/all_gather | solution.py:17
  165.6 2.6 while.34
  168.2 1.3 fusion.43
  170.2 73.0 %all-reduce.34.cloned.1.call-done = f32[256,1024]{1,0:T(8,128)} async-done(((f32[256,1024]{1,0:T(8,128)}), f32[256,1024]{1,0:T(8,128)}) %all-reduce.34.cloned.1.call-update) | async-done | bytes 1048592 | tf_op jit(solution)/shard_map/psum | solution.py:92
  243.2 1.4 fusion.35
  244.6 0.9 gather_fusion
  245.5 61.3 %all-gather.9.cloned.1.call-done = bf16[1024,512]{1,0:T(8,128)(2,1)} async-done(((bf16[16,512]{1,0:T(8,128)(2,1)}), bf16[1024,512]{1,0:T(8,128)(2,1)}) %all-gather.9.cloned.1.call-update) | async-done | bytes 1048592 | tf_op jit(solution)/shard_map/all_gather | solution.py:102
  306.7 2.2 fusion.31
  310.3 1.3 stack.2
  311.6 11.5 %all-to-all-start = ((bf16[64,64,128]{2,1,0:T(8,128)(2,1)}), bf16[64,64,128]{2,1,0:T(8,128)(2,1)S(1)}, u32[]{:S(2)}, u32[]{:S(2)}) async-start(bf16[64,64,128]{2,1,0:T(8,128)(2,1)} %stack.2), calls=%async_computation | async-start | bytes 2097152 | tf_op jit(solution)/shard_map/all_to_all | solution.py:117
  323.2 13.9 %all-gather.11.cloned.1.call-done = bf16[128,4096]{1,0:T(8,128)(2,1)} async-done(((bf16[128,512]{1,0:T(8,128)(2,1)}), bf16[128,4096]{1,0:T(8,128)(2,1)}) %all-gather.11.cloned.1.call-update) | async-done | bytes 1048592 | tf_op jit(solution)/shard_map/all_gather | solution.py:106
  337.1 1.6 fusion.28
  338.8 140.2 %all-gather.17.cloned.1.call-done = bf16[4096,128]{1,0:T(8,128)(2,1)} async-done(((bf16[64,128]{1,0:T(8,128)(2,1)}), bf16[4096,128]{1,0:T(8,128)(2,1)}) %all-gather.17.cloned.1.call-update) | async-done | bytes 1048592 | tf_op jit(solution)/shard_map/all_gather | solution.py:123
  478.9 2.7 convolution_convert_fusion.2
  481.7 1.1 convolution_convert_fusion.3
  483.2 1.3 fusion.50
  485.2 1.9 add_select_fusion.3
  487.8 135.6 %all-gather.15.cloned.1.call-done = bf16[4096,512]{1,0:T(8,128)(2,1)} async-done(((bf16[64,512]{1,0:T(8,128)(2,1)}), bf16[4096,512]{1,0:T(8,128)(2,1)}) %all-gather.15.cloned.1.call-update) | async-done | bytes 4194320 | tf_op jit(solution)/shard_map/all_gather | solution.py:111
  623.5 2.9 convolution_convert_fusion.1
  626.5 135.9 %all-gather.19.cloned.1.call-done = bf16[8192,128]{1,0:T(8,128)(2,1)} async-done(((bf16[128,128]{1,0:T(8,128)(2,1)}), bf16[8192,128]{1,0:T(8,128)(2,1)}) %all-gather.19.cloned.1.call-update) | async-done | bytes 2097168 | tf_op jit(solution)/shard_map/all_gather | solution.py:172
  762.4 139.9 %all-gather.13.cloned.1.call-done = bf16[8192,128]{1,0:T(8,128)(2,1)} async-done(((bf16[128,128]{1,0:T(8,128)(2,1)}), bf16[8192,128]{1,0:T(8,128)(2,1)}) %all-gather.13.cloned.1.call-update) | async-done | bytes 2097168 | tf_op jit(solution)/shard_map/all_gather | solution.py:171
  902.3 50.0 %while.35 = (s32[]{:T(128)}, f32[1,512]{1,0:T(1,128)S(1)}, f32[1,512]{1,0:T(1,128)S(1)}, f32[1,512,128]{2,1,0:T(8,128)S(1)}, s32[64]{0:T(128)S(1)}, /*index=5*/s...) while((s32[]{:T(128)}, f32[1,512]{1,0:T(1,128)S(1)}, ...), condition=%wide.region_13.14_spmd.clone, body=%wide.region_8.13_spmd.clone.sunk | while | flops 273186304 | bytes 7548097 | solution.py:185
  902.3 0.8 fusion.77
  904.0 2.0 fusion.78
  907.0 1.5 fusion.82
  910.2 2.0 fusion.78
  913.3 1.5 fusion.82
  916.5 2.0 fusion.78
  919.5 1.5 fusion.82
  922.7 2.0 fusion.78
  925.8 1.5 fusion.82
  929.0 2.0 fusion.78
  932.0 1.5 fusion.82
  933.5 0.8 fusion.77
  935.2 2.0 fusion.78
  938.3 1.5 fusion.82
  941.5 2.0 fusion.78
  944.5 1.5 fusion.82
  947.7 2.0 fusion.78
  950.8 1.5 fusion.82
  952.8 0.8 copy.28
  953.7 35.8 %reduce-scatter.4.cloned.1.call-done = bf16[128,128]{1,0:T(8,128)(2,1)} async-done(((bf16[1024,128]{1,0:T(8,128)(2,1)}), bf16[128,128]{1,0:T(8,128)(2,1)}) %reduce-scatter.4.cloned.1.call-update) | async-done | bytes 32784
  989.6 0.9 copy.29
  990.4 0.9 gather_fusion.1
  991.3 1.5 add_convert_fusion
  (337 shorter events, 27.7 us)
Async XLA Ops:
  7.4 945.1 %copy-start = (bf16[512,1024]{1,0:T(8,128)(2,1)S(1)}, bf16[512,1024]{1,0:T(8,128)(2,1)}, u32[]{:S(2)}) copy-start(bf16[512,1024]{1,0:T(8,128)(2,1)} %param.33) | copy-start | bytes 3145732
  7.4 3.0 copy-start.2
  7.4 3.0 copy-start.13
  7.4 3.0 copy-start.11
  7.4 235.8 %all-reduce.34.cloned.1.call-start = ((), (), s32[]{:S(2)}) async-start(), calls=%async_computation.2 | async-start | bytes 2097152 | tf_op jit(solution)/shard_map/psum | solution.py:92
  11.7 156.5 %copy-start.4 = (bf16[128,1024]{1,0:T(8,128)(2,1)S(1)}, bf16[128,1024]{1,0:T(8,128)(2,1)}, u32[]{:S(2)}) copy-start(bf16[128,1024]{1,0:T(8,128)(2,1)} %param.24) | copy-start | bytes 786436
  12.5 157.6 %copy-start.10 = (s32[1,128]{1,0:T(1,128)S(1)}, s32[1,128]{1,0:T(1,128)}, u32[]{:S(2)}) copy-start(s32[1,128]{1,0:T(1,128)} %param.25) | copy-start | bytes 1540
  169.5 137.2 %all-gather.9.cloned.1.call-start = ((), (), s32[]{:S(2)}) async-start(), calls=%async_computation.3 | async-start | bytes 1064960 | tf_op jit(solution)/shard_map/all_gather | solution.py:102
  170.1 167.0 %all-gather.11.cloned.1.call-start = ((), (), s32[]{:S(2)}) async-start(), calls=%async_computation.4 | async-start | bytes 1179648 | tf_op jit(solution)/shard_map/all_gather | solution.py:106
  170.2 136.5 %copy-start.9 = (f32[512]{0:T(512)S(1)}, f32[512]{0:T(512)}, u32[]{:S(2)}) copy-start(f32[512]{0:T(512)} %param.28) | copy-start | bytes 6148
  244.6 67.0 %copy-start.1 = (bf16[256,1024]{1,0:T(8,128)(2,1)}, bf16[256,1024]{1,0:T(8,128)(2,1)S(1)}, u32[]{:S(2)}) copy-start(bf16[256,1024]{1,0:T(8,128)(2,1)S(1)} %fusion.35) | copy-start | bytes 1572868
  244.6 65.7 %copy-start.7 = (bf16[64,128]{1,0:T(8,128)(2,1)S(1)}, bf16[64,128]{1,0:T(8,128)(2,1)}, u32[]{:S(2)}) copy-start(bf16[64,128]{1,0:T(8,128)(2,1)} %param.31) | copy-start | bytes 49156
  309.0 170.0 %all-gather.17.cloned.1.call-start = ((), (), s32[]{:S(2)}) async-start(), calls=%async_computation.7 | async-start | bytes 1064960 | tf_op jit(solution)/shard_map/all_gather | solution.py:123
  309.7 313.8 %all-gather.15.cloned.1.call-start = ((), (), s32[]{:S(2)}) async-start(), calls=%async_computation.6 | async-start | bytes 4259840 | tf_op jit(solution)/shard_map/all_gather | solution.py:111
  310.3 168.7 %copy-start.12 = (f32[4096]{0:T(1024)S(1)}, f32[4096]{0:T(1024)}, u32[]{:S(2)}) copy-start(f32[4096]{0:T(1024)} %param.29) | copy-start | bytes 49156
  311.6 170.1 %all-to-all-start = ((bf16[64,64,128]{2,1,0:T(8,128)(2,1)}), bf16[64,64,128]{2,1,0:T(8,128)(2,1)S(1)}, u32[]{:S(2)}, u32[]{:S(2)}) async-start(bf16[64,64,128]{2,1,0:T(8,128)(2,1)} %stack.2), calls=%async_computation | async-start | bytes 2097152 | tf_op jit(solution)/shard_map/all_to_all | solution.py:117
  323.1 439.3 %all-gather.19.cloned.1.call-start = ((), (), s32[]{:S(2)}) async-start(), calls=%async_computation.8 | async-start | bytes 2129920 | tf_op jit(solution)/shard_map/all_gather | solution.py:172
  337.1 144.6 %copy-start.3 = (bf16[128,4096]{1,0:T(8,128)(2,1)S(1)}, bf16[128,4096]{1,0:T(8,128)(2,1)}, u32[]{:S(2)}) copy-start(bf16[128,4096]{1,0:T(8,128)(2,1)} %all-gather.11.cloned.1.call-done) | copy-start | bytes 3145732
  338.7 144.2 %copy-start.5 = (s32[64]{0:T(128)S(1)}, s32[64]{0:T(128)}, u32[]{:S(2)}) copy-start(s32[64]{0:T(128)} %param.26) | copy-start | bytes 772
  481.6 420.7 %all-gather.13.cloned.1.call-start = ((), (), s32[]{:S(2)}) async-start(), calls=%async_computation.5 | async-start | bytes 2129920 | tf_op jit(solution)/shard_map/all_gather | solution.py:171
  482.8 506.7 %reduce-scatter.4.cloned.1.call-start = ((), (), s32[]{:S(2)}) async-start(), calls=%async_computation.9 | async-start | bytes 294912
  906.7 1.9 copy-start.6
  912.9 1.9 copy-start.6
  919.2 1.9 copy-start.6
  925.4 1.9 copy-start.6
  931.6 1.9 copy-start.6
  937.9 1.9 copy-start.6
  944.1 1.9 copy-start.6
  950.4 1.9 copy-start.6
  952.3 1.4 copy-start.8
Sparse Core Ops, SparseCore 0:
  169.7 73.5 all-reduce.33
  309.1 28.0 all-gather.10
  340.1 138.8 all-gather.16
  481.7 141.6 all-gather.14
  626.2 136.1 all-gather.18
  765.2 137.0 all-gather.12
  953.8 35.6 reduce-scatter.3
Sparse Core Ops, SparseCore 1:
  173.0 133.7 all-gather.8
